TPU v7x, 256 devices: a whole 4x4x8 slice. The times are simulated.
256 devices in a mesh: band: 64 (over x, z, core), lev: 4 (over y).
Axes of the slice: x: 4, y: 4, z: 8, core: 2. Of those that a mesh axis runs over, the one named last changes fastest.
Arguments:
- obs_vals: bfloat16 [4, 24, 262144], P('lev', None, 'band'), may hold values from -400 to 400
- obs_colat: bfloat16 [262144], P('band'), may hold values from -1 to 1
- obs_lon: int32 [262144], P('band'), may hold values from 0 to 2047
- band_list: int32 [64, 64, 128], P('band'), may hold values from 0 to 4095, as said below
- counts: int32 [64, 64], P('band'), may hold values from 0 to 128, as said below
- w_in: bfloat16 [96, 256], replicated, may hold values from -0.625 to 0.625
- b_in: float32 [256], replicated, may hold values from -3 to 3
- w_out: bfloat16 [256, 256], P(None, 'lev'), may hold values from -0.375 to 0.375
- b_out: float32 [256], P('lev'), may hold values from -3 to 3
Outputs:
- encoded: bfloat16 [256, 2048, 512], P('lev', 'band')
Inputs may be any that keep to these rules, and one draw needn't show every extreme that they name: For each device s and band b the first counts[s, b] entries of band_list[s, b] are indices (within device s) of observations in band b; over all b they name every observation of device s exactly once. Later entries are padding and name arbitrary observations. `counts`: each row sums to 4096. Some band receives 128 observations from every device.
All inputs are finite; a program needn't handle non-finite values.
Results may differ from a plain program's by a relative error of at most 0.0063.
Values may be sent and summed in bfloat16 or wider, within the bound.
A program may use at most 64 MiB of HBM per device.

v0:
```python
import math
import jax
import jax.numpy as jnp
from jax import lax
from jax.sharding import PartitionSpec as P

LAT_DEV = 8
LON_DEV = 32
norm_eps = 1e-05


def cheb_inverse(nodes):
    order_ids = jnp.arange(nodes, dtype=jnp.float32)[:, None]
    node_ids = jnp.arange(nodes, dtype=jnp.float32)[None, :]
    factor = jnp.where(order_ids == 0.0, 1.0, 2.0).astype(jnp.float32) / nodes
    return factor * jnp.cos(math.pi * order_ids * (node_ids + 0.5) / nodes)


def lat_weights(colat, nodes):
    angles = jnp.arccos(jnp.clip(colat, -1.0, 1.0))
    order_ids = jnp.arange(nodes, dtype=jnp.float32)
    cheb_terms = jnp.cos(order_ids[:, None] * angles[None, :])
    return jnp.dot(cheb_inverse(nodes).T, cheb_terms, precision=lax.Precision.HIGHEST)


def dct_table(length):
    mode_ids = jnp.arange(length, dtype=jnp.float32)[:, None]
    node_ids = jnp.arange(length, dtype=jnp.float32)[None, :]
    row_scale = jnp.where(mode_ids == 0.0, math.sqrt(1.0 / length), math.sqrt(2.0 / length)).astype(
        jnp.float32
    )
    return (row_scale * jnp.cos(math.pi * mode_ids * (node_ids + 0.5) / length)).astype(
        jnp.bfloat16
    )


def on_device(obs_vals, obs_colat, obs_lon, band_list, counts, w_in, b_in, w_out, b_out):
    band_count = lax.axis_size("band")
    capacity = band_list.shape[2]
    lat_nodes = LAT_DEV
    lon_local = LON_DEV
    lon_count = lon_local * band_count
    lat_total = lat_nodes * band_count
    channels = obs_vals.shape[1]
    feat_count = w_in.shape[0]
    picked = band_list[0].reshape(-1)
    live_slot = (jnp.arange(capacity, dtype=jnp.int32)[None, :] < counts[0][:, None]).reshape(-1)
    outgoing = jnp.where(
        live_slot[None, :], jnp.take(obs_vals[0], picked, axis=1), jnp.zeros((), jnp.bfloat16)
    )
    colat_out = jnp.take(obs_colat, picked)[None, :]
    lon_out = jnp.take(obs_lon, picked)[None, :]
    incoming, colat_in, lon_in = (
        lax.all_to_all(outgoing, "band", split_axis=1, concat_axis=1, tiled=True),
        lax.all_to_all(colat_out, "band", split_axis=1, concat_axis=1, tiled=True),
        lax.all_to_all(lon_out, "band", split_axis=1, concat_axis=1, tiled=True),
    )
    weights = lat_weights(colat_in[0].astype(jnp.float32), lat_nodes)
    weighted = (incoming.astype(jnp.float32)[:, None, :] * weights[None]).astype(jnp.bfloat16)
    weighted = weighted.reshape(channels * lat_nodes, -1)
    lon_ids = lon_in[0]
    row_count = weighted.shape[1]
    block_rows = math.gcd(row_count, 1024)
    columns = jnp.arange(lon_count, dtype=jnp.int32)

    def add_block(step_index, grid_sum):
        first_row = step_index * block_rows
        block_vals = lax.dynamic_slice_in_dim(weighted, first_row, block_rows, 1)
        block_lon = lax.dynamic_slice_in_dim(lon_ids, first_row, block_rows, 0)
        onehot = (block_lon[:, None] == columns[None, :]).astype(jnp.bfloat16)
        return grid_sum + jnp.dot(block_vals, onehot, preferred_element_type=jnp.float32)

    grid_sum = lax.fori_loop(
        0,
        row_count // block_rows,
        add_block,
        jnp.zeros((channels * lat_nodes, lon_count), jnp.float32),
    )
    grid_half = grid_sum.astype(jnp.bfloat16).reshape(channels, lat_nodes, lon_count)
    all_levels = lax.all_gather(grid_half, "lev", axis=0, tiled=True)
    received = lax.all_to_all(all_levels, "band", split_axis=2, concat_axis=2, tiled=True)
    items = received.shape[0]
    arranged = received.reshape(items, lat_nodes, band_count, lon_local)
    table = dct_table(lat_total).reshape(lat_total, band_count, lat_nodes)
    spectrum = jnp.einsum(
        "cjbm,kbj->cmk", arranged, table, preferred_element_type=jnp.float32
    ).astype(jnp.bfloat16)
    pre_act = jnp.einsum("fh,fmk->hmk", w_in, spectrum, preferred_element_type=jnp.float32)
    squared = spectrum.astype(jnp.float32)
    pre_act, sum_sq = (pre_act, jnp.sum(squared * squared, axis=0))
    inv_norm = lax.rsqrt(sum_sq * (1.0 / feat_count) + norm_eps)
    hidden = jax.nn.gelu(pre_act * inv_norm[None] + b_in[:, None, None]).astype(jnp.bfloat16)
    output = (
        jnp.einsum("ho,hmk->omk", w_out, hidden, preferred_element_type=jnp.float32)
        + b_out[:, None, None]
    )
    return output.astype(jnp.bfloat16)


def solution(mesh):
    in_specs = (
        P("lev", None, "band"),
        P("band"),
        P("band"),
        P("band", None, None),
        P("band", None),
        P(),
        P(),
        P(None, "lev"),
        P("lev"),
    )
    out_specs = P("lev", "band", None)
    return jax.shard_map(
        on_device, mesh=mesh, in_specs=in_specs, out_specs=out_specs, check_vma=False
    )
```

profile of v0, /device:TPU:1, one launch (start us, length us, event | category | flops | bytes accessed | tf_op | source)
XLA Modules:
  0.0 420.4 jit_solution(8596966610472597191)
XLA Ops:
  6.5 0.8 compare_select_fusion
  7.4 45.5 %gather_fusion.2 = s32[8192]{0:T(1024)S(1)} fusion(s32[4096]{0:T(1024)S(1)} %copy-done.1, s32[8192]{0:T(1024)S(1)} %broadcast_clamp_fusion), kind=kCustom, calls=%fused_computation.2 | custom fusion | bytes 98304 | tf_op jit(solution)/shard_map/jit(_take)/gather | solution.py:52
  53.0 0.6 bitcast_select_fusion
  53.6 50.7 %gather_fusion.1 = bf16[8192]{0:T(1024)(128)(2,1)S(1)} fusion(bf16[4096]{0:T(1024)(128)(2,1)S(1)} %copy-done.2, s32[8192]{0:T(1024)S(1)} %broadcast_clamp_fusion), kind=kCustom, calls=%fused_computation.1 | custom fusion | bytes 65536 | tf_op jit(solution)/shard_map/jit(_take)/gather | solution.py:51
  104.4 0.6 copy.55
  105.0 13.0 %all-to-all-start.1 = ((bf16[1,64,128]{2,0,1:T(2,128)(2,1)}), bf16[1,64,128]{2,0,1:T(2,128)(2,1)S(1)}, u32[]{:S(2)}, u32[]{:S(2)}) async-start(bf16[1,64,128]{2,0,1:T(2,128)(2,1)} %copy.55), calls=%async_computation.1 | async-start | bytes 65536 | tf_op jit(solution)/shard_map/all_to_all | solution.py:55
  118.5 24.0 %gather_fusion = bf16[8192,24]{1,0:T(8,128)(2,1)S(1)} fusion(bf16[24,4096]{0,1:T(8,128)(2,1)S(1)} %bitcast.52, s32[8192]{0:T(1024)S(1)} %broadcast_clamp_fusion), kind=kCustom, calls=%fused_computation | custom fusion | bytes 819200 | tf_op jit(solution)/shard_map/jit(_take)/gather | solution.py:49
  142.6 0.9 copy.53
  143.5 0.9 select_select_fusion
  144.4 10.3 %all-to-all-start = ((bf16[24,64,128]{2,0,1:T(8,128)(2,1)}), bf16[24,64,128]{2,0,1:T(8,128)(2,1)S(1)}, u32[]{:S(2)}, u32[]{:S(2)}) async-start(bf16[24,64,128]{2,0,1:T(8,128)(2,1)} %select_select_fusion), calls=%async_computation | async-start | bytes 786432 | tf_op jit(solution)/shard_map/all_to_all | solution.py:54
  154.9 1.2 fusion.29
  156.1 13.2 %all-to-all-done = bf16[24,64,128]{2,0,1:T(8,128)(2,1)S(1)} async-done(((bf16[24,64,128]{2,0,1:T(8,128)(2,1)}), bf16[24,64,128]{2,0,1:T(8,128)(2,1)S(1)}, u32[]{:S(2)}, u32[]{:S(2)}) %all-to-all-start) | async-done | bytes 393248 | tf_op jit(solution)/shard_map/all_to_all | solution.py:54
  169.3 6.2 %all-to-all-start.2 = ((s32[1,64,128]{2,0,1:T(1,128)}), s32[1,64,128]{2,0,1:T(1,128)S(1)}, u32[]{:S(2)}, u32[]{:S(2)}) async-start(s32[1,64,128]{2,0,1:T(1,128)} %bitcast.11), calls=%async_computation.2 | async-start | bytes 65536 | tf_op jit(solution)/shard_map/all_to_all | solution.py:56
  176.1 8.7 %all-to-all-done.2 = s32[1,64,128]{2,0,1:T(1,128)S(1)} async-done(((s32[1,64,128]{2,0,1:T(1,128)}), s32[1,64,128]{2,0,1:T(1,128)S(1)}, u32[]{:S(2)}, u32[]{:S(2)}) %all-to-all-start.2) | async-done | bytes 32800 | tf_op jit(solution)/shard_map/all_to_all | solution.py:56
  184.9 35.6 %while.14 = (s32[]{:T(128)}, f32[192,2048]{1,0:T(8,128)}, bf16[192,8192]{1,0:T(8,128)(2,1)S(1)}, s32[8192]{0:T(1024)S(1)}, s32[]{:T(128)}, /*index=5*/s32[]{:T(128)}, s32[]{:T(128)}, s32[]{:T(128)}) while((s32[]{:T(128)}, f32[192,2048]{1,0:T(8,128)}, bf16[192,8192]{1,0:T(8,128)(2,1)S(1)}, s32[8192]{0:T(1024)S(1)}, s32[]{:T(128)}, ...), condition=%wide.region_1.2_spmd.clone, body=%wide.region_0.1_spmd.clone.sunk | while | flops 808189952 | bytes 3551381 | solution.py:73
  184.9 3.2 fusion.57
  188.1 4.6 %fusion.57 = f32[192,2048]{1,0:T(8,128)} fusion(s32[1024]{0:T(1024)S(1)} %dynamic_slice.21, f32[192,2048]{1,0:T(8,128)} %get-tuple-element.167, pred[]{:T(512)S(6)} %compare.3, bf16[192,8192]{1,0:T(8,128)(2,1)S(1)} %get-tuple-element.176, s32[]{:T(128)S(6)} %select_n.102), kind=kOutput, calls=%fused_computation.7.clone.1 | convolution fusion | flops 808189952 | bytes 3543045 | tf_op jit(solution)/shard_map/while/body/eval_jaxpr/dot_general | solution.py:71
  192.7 4.6 %fusion.57 = f32[192,2048]{1,0:T(8,128)} fusion(s32[1024]{0:T(1024)S(1)} %dynamic_slice.21, f32[192,2048]{1,0:T(8,128)} %get-tuple-element.167, pred[]{:T(512)S(6)} %compare.3, bf16[192,8192]{1,0:T(8,128)(2,1)S(1)} %get-tuple-element.176, s32[]{:T(128)S(6)} %select_n.102), kind=kOutput, calls=%fused_computation.7.clone.1 | convolution fusion | flops 808189952 | bytes 3543045 | tf_op jit(solution)/shard_map/while/body/eval_jaxpr/dot_general | solution.py:71
  197.3 4.6 %fusion.57 = f32[192,2048]{1,0:T(8,128)} fusion(s32[1024]{0:T(1024)S(1)} %dynamic_slice.21, f32[192,2048]{1,0:T(8,128)} %get-tuple-element.167, pred[]{:T(512)S(6)} %compare.3, bf16[192,8192]{1,0:T(8,128)(2,1)S(1)} %get-tuple-element.176, s32[]{:T(128)S(6)} %select_n.102), kind=kOutput, calls=%fused_computation.7.clone.1 | convolution fusion | flops 808189952 | bytes 3543045 | tf_op jit(solution)/shard_map/while/body/eval_jaxpr/dot_general | solution.py:71
  202.0 4.6 %fusion.57 = f32[192,2048]{1,0:T(8,128)} fusion(s32[1024]{0:T(1024)S(1)} %dynamic_slice.21, f32[192,2048]{1,0:T(8,128)} %get-tuple-element.167, pred[]{:T(512)S(6)} %compare.3, bf16[192,8192]{1,0:T(8,128)(2,1)S(1)} %get-tuple-element.176, s32[]{:T(128)S(6)} %select_n.102), kind=kOutput, calls=%fused_computation.7.clone.1 | convolution fusion | flops 808189952 | bytes 3543045 | tf_op jit(solution)/shard_map/while/body/eval_jaxpr/dot_general | solution.py:71
  206.6 4.6 %fusion.57 = f32[192,2048]{1,0:T(8,128)} fusion(s32[1024]{0:T(1024)S(1)} %dynamic_slice.21, f32[192,2048]{1,0:T(8,128)} %get-tuple-element.167, pred[]{:T(512)S(6)} %compare.3, bf16[192,8192]{1,0:T(8,128)(2,1)S(1)} %get-tuple-element.176, s32[]{:T(128)S(6)} %select_n.102), kind=kOutput, calls=%fused_computation.7.clone.1 | convolution fusion | flops 808189952 | bytes 3543045 | tf_op jit(solution)/shard_map/while/body/eval_jaxpr/dot_general | solution.py:71
  211.2 4.6 %fusion.57 = f32[192,2048]{1,0:T(8,128)} fusion(s32[1024]{0:T(1024)S(1)} %dynamic_slice.21, f32[192,2048]{1,0:T(8,128)} %get-tuple-element.167, pred[]{:T(512)S(6)} %compare.3, bf16[192,8192]{1,0:T(8,128)(2,1)S(1)} %get-tuple-element.176, s32[]{:T(128)S(6)} %select_n.102), kind=kOutput, calls=%fused_computation.7.clone.1 | convolution fusion | flops 808189952 | bytes 3543045 | tf_op jit(solution)/shard_map/while/body/eval_jaxpr/dot_general | solution.py:71
  215.9 4.6 %fusion.57 = f32[192,2048]{1,0:T(8,128)} fusion(s32[1024]{0:T(1024)S(1)} %dynamic_slice.21, f32[192,2048]{1,0:T(8,128)} %get-tuple-element.167, pred[]{:T(512)S(6)} %compare.3, bf16[192,8192]{1,0:T(8,128)(2,1)S(1)} %get-tuple-element.176, s32[]{:T(128)S(6)} %select_n.102), kind=kOutput, calls=%fused_computation.7.clone.1 | convolution fusion | flops 808189952 | bytes 3543045 | tf_op jit(solution)/shard_map/while/body/eval_jaxpr/dot_general | solution.py:71
  220.5 2.4 convert_bitcast_fusion.1
  222.9 36.9 %all-gather.2.cloned.1.call-done = bf16[96,8,2048]{2,1,0:T(8,128)(2,1)} async-done(((bf16[24,8,2048]{2,1,0:T(8,128)(2,1)}), bf16[96,8,2048]{2,1,0:T(8,128)(2,1)}) %all-gather.2.cloned.1.call-update) | async-done | bytes 3145744 | tf_op jit(solution)/shard_map/all_gather | solution.py:80
  259.9 7.0 %copy.57 = bf16[96,8,2048]{0,1,2:T(8,128)(2,1)} copy(bf16[96,8,2048]{2,1,0:T(8,128)(2,1)} %all-gather.2.cloned.1.call-done) | data formatting | bytes 6291456 | tf_op jit(solution)/shard_map/all_gather | solution.py:80
  266.9 11.0 %all-to-all-start.3 = ((bf16[96,8,2048]{0,1,2:T(8,128)(2,1)}), bf16[96,8,2048]{0,1,2:T(8,128)(2,1)}, u32[]{:S(2)}, u32[]{:S(2)}) async-start(bf16[96,8,2048]{0,1,2:T(8,128)(2,1)} %copy.57), calls=%async_computation.3 | async-start | bytes 8388608 | tf_op jit(solution)/shard_map/all_to_all | solution.py:81
  277.9 95.8 %all-to-all-done.3 = bf16[96,8,2048]{0,1,2:T(8,128)(2,1)} async-done(((bf16[96,8,2048]{0,1,2:T(8,128)(2,1)}), bf16[96,8,2048]{0,1,2:T(8,128)(2,1)}, u32[]{:S(2)}, u32[]{:S(2)}) %all-to-all-start.3) | async-done | bytes 3145760 | tf_op jit(solution)/shard_map/all_to_all | solution.py:81
  373.7 13.4 %copy.59 = bf16[96,8,64,32]{2,3,1,0:T(8,128)(2,1)} copy(bf16[96,8,64,32]{0,1,3,2:T(8,128)(2,1)} %bitcast.14) | data formatting | bytes 6291456 | tf_op jit(solution)/shard_map/reshape | solution.py:83
  387.1 11.2 %multiply_reduce_fusion = (f32[32,512]{1,0:T(8,128)S(1)}, bf16[96,32,512]{2,1,0:T(8,128)(2,1)}) fusion(bf16[96,8,64,32]{2,3,1,0:T(8,128)(2,1)} %copy.59, f32[64,8]{0,1:T(8,128)S(1)} %add_add_fusion, f32[512]{0:T(512)S(1)} %get-tuple-element.131, f32[512]{0:T(512)S(1)} %get-tuple-element.132), kind=kOutput, calls=%fused_computation.20 | convolution fusion | flops 1617936384 | bytes 6363136 | tf_op jit(solution)/shard_map/cjbm,kbj->cmk/dot_general | solution.py:85
  398.3 12.7 %fusion.20 = bf16[64,32,512]{2,0,1:T(8,128)(2,1)S(1)} fusion(f32[64]{0:T(128)S(1)} %copy-done.8, f32[256]{0:T(256)S(1)} %copy-done.7, f32[32,512]{1,0:T(8,128)S(1)} %add_rsqrt_fusion, bf16[96,32,512]{2,1,0:T(8,128)(2,1)} %get-tuple-element.128, bf16[96,256]{1,0:T(8,128)(2,1)S(1)} %copy-done, bf16[256,64]{0,1:T(8,128)(2,1)S(1)} %copy-done.6), kind=kOutput, calls=%fused_computation.26 | convolution fusion | flops 1390411776 | bytes 5391616 | tf_op jit(solution)/shard_map/ho,hmk->omk/dot_general | solution.py:94
  411.0 2.5 copy.62
  (44 shorter events, 1.4 us)
Async XLA Ops:
  6.5 391.7 %copy-start = (bf16[96,256]{1,0:T(8,128)(2,1)S(1)}, bf16[96,256]{1,0:T(8,128)(2,1)}, u32[]{:S(2)}) copy-start(bf16[96,256]{1,0:T(8,128)(2,1)} %param.16) | copy-start | bytes 147460
  6.5 0.8 copy-start.1
  7.4 45.6 %copy-start.3 = (s32[1,64,128]{2,1,0:T(8,128)S(1)}, s32[1,64,128]{2,1,0:T(8,128)}, u32[]{:S(2)}) copy-start(s32[1,64,128]{2,1,0:T(8,128)} %param.14) | copy-start | bytes 98308
  52.9 0.7 copy-start.2
  53.6 64.4 %copy-start.4 = (bf16[1,24,4096]{2,1,0:T(8,128)(2,1)S(1)}, bf16[1,24,4096]{2,1,0:T(8,128)(2,1)}, u32[]{:S(2)}) copy-start(bf16[1,24,4096]{2,1,0:T(8,128)(2,1)} %param.11) | copy-start | bytes 589828
  104.4 39.1 %copy-start.5 = (s32[1,64]{1,0:T(1,128)S(1)}, s32[1,64]{1,0:T(1,128)}, u32[]{:S(2)}) copy-start(s32[1,64]{1,0:T(1,128)} %param.15) | copy-start | bytes 772
  105.0 39.4 %all-to-all-start.1 = ((bf16[1,64,128]{2,0,1:T(2,128)(2,1)}), bf16[1,64,128]{2,0,1:T(2,128)(2,1)S(1)}, u32[]{:S(2)}, u32[]{:S(2)}) async-start(bf16[1,64,128]{2,0,1:T(2,128)(2,1)} %copy.55), calls=%async_computation.1 | async-start | bytes 65536 | tf_op jit(solution)/shard_map/all_to_all | solution.py:55
  144.4 24.9 %all-to-all-start = ((bf16[24,64,128]{2,0,1:T(8,128)(2,1)}), bf16[24,64,128]{2,0,1:T(8,128)(2,1)S(1)}, u32[]{:S(2)}, u32[]{:S(2)}) async-start(bf16[24,64,128]{2,0,1:T(8,128)(2,1)} %select_select_fusion), calls=%async_computation | async-start | bytes 786432 | tf_op jit(solution)/shard_map/all_to_all | solution.py:54
  169.3 15.6 %all-to-all-start.2 = ((s32[1,64,128]{2,0,1:T(1,128)}), s32[1,64,128]{2,0,1:T(1,128)S(1)}, u32[]{:S(2)}, u32[]{:S(2)}) async-start(s32[1,64,128]{2,0,1:T(1,128)} %bitcast.11), calls=%async_computation.2 | async-start | bytes 65536 | tf_op jit(solution)/shard_map/all_to_all | solution.py:56
  175.5 84.3 %all-gather.2.cloned.1.call-start = ((), (), s32[]{:S(2)}) async-start(), calls=%async_computation.4 | async-start | bytes 3932160 | tf_op jit(solution)/shard_map/all_gather | solution.py:80
  266.9 106.9 %all-to-all-start.3 = ((bf16[96,8,2048]{0,1,2:T(8,128)(2,1)}), bf16[96,8,2048]{0,1,2:T(8,128)(2,1)}, u32[]{:S(2)}, u32[]{:S(2)}) async-start(bf16[96,8,2048]{0,1,2:T(8,128)(2,1)} %copy.57), calls=%async_computation.3 | async-start | bytes 8388608 | tf_op jit(solution)/shard_map/all_to_all | solution.py:81
  387.1 11.2 %copy-start.6 = (bf16[256,64]{0,1:T(8,128)(2,1)S(1)}, bf16[256,64]{0,1:T(8,128)(2,1)}, u32[]{:S(2)}) copy-start(bf16[256,64]{0,1:T(8,128)(2,1)} %param.18) | copy-start | bytes 98308
  387.1 11.2 %copy-start.7 = (f32[256]{0:T(256)S(1)}, f32[256]{0:T(256)}, u32[]{:S(2)}) copy-start(f32[256]{0:T(256)} %param.17) | copy-start | bytes 3076
  387.1 11.2 %copy-start.8 = (f32[64]{0:T(128)S(1)}, f32[64]{0:T(128)}, u32[]{:S(2)}) copy-start(f32[64]{0:T(128)} %param.19) | copy-start | bytes 772
Sparse Core Ops, SparseCore 0:
  223.1 36.7 all-gather.1
where the time goes:
time: 421 us; the launch traced here: 420 us
  waiting for transfers between devices  155 us (37%)
  local copies, waits for them, and re-layouts  145 us (34%)
  matrix products  60.7 us (14%)
  starting transfers between devices  40.6 us (10%)
  between operations  13.7 us (3%)
  other arithmetic  5.5 us (1%)
    all_to_all x1, waiting for transfers between devices, on_device(): lax.all_to_all(all_levels, 'band', split_axis=2, concat_axis=2, tiled=True)  95.8 us
    gather x1, local copies, waits for them, and re-layouts, on_device(): colat_out = jnp.take(obs_colat, picked)[None, :]  50.7 us
    gather x1, local copies, waits for them, and re-layouts, on_device(): lon_out = jnp.take(obs_lon, picked)[None, :]  45.5 us
    all_gather x1, waiting for transfers between devices, on_device(): all_levels = lax.all_gather(grid_half, 'lev', axis=0, tiled=True)  36.9 us
    dot_general x8, matrix products, add_block(): jnp.dot(block_vals, onehot, preferred_element_type=jnp.float32)  35.6 us
    gather x2, local copies, waits for them, and re-layouts, on_device(): jnp.take(obs_vals[0], picked, axis=1)  24.9 us
    reshape x1, local copies, waits for them, and re-layouts, on_device(): arranged = received.reshape(items, lat_nodes, band_count, lon_local)  13.4 us
    all_to_all x1, waiting for transfers between devices, on_device(): lax.all_to_all(outgoing, 'band', split_axis=1, concat_axis=1, tiled=True)  13.2 us
  transfers between devices with their start and end apart: 5, of which 4 were waited for; matrix products, arithmetic and copies ran while one was open for 7% of the time, Pallas kernels for 0%

commit v1 on v0

--- a/solution.py
+++ b/solution.py
@@ -35,6 +35,15 @@
 
 
 def on_device(obs_vals, obs_colat, obs_lon, band_list, counts, w_in, b_in, w_out, b_out):
+
+    def groups_replace(local_array, across, d0):
+        return jnp.concatenate(
+            jax.lax.all_to_all(
+                jnp.stack([local_array for _ in range(jax.lax.axis_size(across))]), across, 0, 0
+            ),
+            axis=d0,
+        )
+
     band_count = lax.axis_size("band")
     capacity = band_list.shape[2]
     lat_nodes = LAT_DEV
@@ -77,7 +86,7 @@
         jnp.zeros((channels * lat_nodes, lon_count), jnp.float32),
     )
     grid_half = grid_sum.astype(jnp.bfloat16).reshape(channels, lat_nodes, lon_count)
-    all_levels = lax.all_gather(grid_half, "lev", axis=0, tiled=True)
+    all_levels = groups_replace(grid_half, "lev", 0)
     received = lax.all_to_all(all_levels, "band", split_axis=2, concat_axis=2, tiled=True)
     items = received.shape[0]
     arranged = received.reshape(items, lat_nodes, band_count, lon_local)

time: 421 us -> 405 us (0.962)
  blocking collectives: 0 us -> 40.7 us
  waiting for transfers between devices: 155 us -> 118 us
  between operations: 13.7 us -> 0.27 us
    all_to_all x0 -> x1, blocking collectives: none -> 40.7 us  [groups_replace(): jax.lax.all_to_all(jnp.stack([local_array for _ in range(jax.lax.axis_siz...]
    all_gather x1 -> x0, waiting for transfers between devices: 36.9 us -> none  [on_device(): all_levels = lax.all_gather(grid_half, 'lev', axis=0, tiled=True)]
    all_gather x1 -> x0, local copies, waits for them, and re-layouts: 7.01 us -> none  [on_device(): all_levels = lax.all_gather(grid_half, 'lev', axis=0, tiled=True)]
    reshape x0 -> x1, local copies, waits for them, and re-layouts: none -> 5.19 us  [groups_replace(): jnp.concatenate(jax.lax.all_to_all(jnp.stack([local_array for _ in range(...]
  transfers between devices with their start and end apart: 5 -> 4, of which waited for: 4 -> 3; matrix products, arithmetic and copies ran while one was open for 7% -> 7% of each run, Pallas kernels for 0% -> 0%
where the time goes in v1:
time: 405 us; the launch traced here: 404 us
  local copies, waits for them, and re-layouts  144 us (36%)
  waiting for transfers between devices  118 us (29%)
  matrix products  60.8 us (15%)
  blocking collectives  40.7 us (10%)
  starting transfers between devices  36.4 us (9%)
  other arithmetic  4.58 us (1%)
    all_to_all x1, waiting for transfers between devices, on_device(): lax.all_to_all(all_levels, 'band', split_axis=2, concat_axis=2, tiled=True)  95.9 us
    gather x1, local copies, waits for them, and re-layouts, on_device(): colat_out = jnp.take(obs_colat, picked)[None, :]  50.7 us
    gather x1, local copies, waits for them, and re-layouts, on_device(): lon_out = jnp.take(obs_lon, picked)[None, :]  45.5 us
    all_to_all x1, blocking collectives, groups_replace(): jax.lax.all_to_all(jnp.stack([local_array for _ in range(jax.lax.axis_siz...  40.7 us
    dot_general x8, matrix products, add_block(): jnp.dot(block_vals, onehot, preferred_element_type=jnp.float32)  35.6 us
    gather x2, local copies, waits for them, and re-layouts, on_device(): jnp.take(obs_vals[0], picked, axis=1)  24.9 us
    reshape x1, local copies, waits for them, and re-layouts, on_device(): arranged = received.reshape(items, lat_nodes, band_count, lon_local)  13.4 us
    all_to_all x1, waiting for transfers between devices, on_device(): lax.all_to_all(outgoing, 'band', split_axis=1, concat_axis=1, tiled=True)  13.2 us
  transfers between devices with their start and end apart: 4, of which 3 were waited for; matrix products, arithmetic and copies ran while one was open for 7% of the time, Pallas kernels for 0%

profile of v1, /device:TPU:1, one launch (start us, length us, event | category | flops | bytes accessed | tf_op | source)
XLA Modules:
  0.0 404.3 jit_solution(15577049272050844059)
XLA Ops:
  0.0 0.8 compare_select_fusion
  0.9 45.5 %gather_fusion.2 = s32[8192]{0:T(1024)S(1)} fusion(s32[4096]{0:T(1024)S(1)} %copy-done.1, s32[8192]{0:T(1024)S(1)} %broadcast_clamp_fusion), kind=kCustom, calls=%fused_computation.2 | custom fusion | bytes 98304 | tf_op jit(solution)/shard_map/jit(_take)/gather | solution.py:61
  46.4 0.6 bitcast_select_fusion
  47.1 50.7 %gather_fusion.1 = bf16[8192]{0:T(1024)(128)(2,1)S(1)} fusion(bf16[4096]{0:T(1024)(128)(2,1)S(1)} %copy-done.2, s32[8192]{0:T(1024)S(1)} %broadcast_clamp_fusion), kind=kCustom, calls=%fused_computation.1 | custom fusion | bytes 65536 | tf_op jit(solution)/shard_map/jit(_take)/gather | solution.py:60
  97.9 0.6 copy.56
  98.5 13.0 %all-to-all-start.1 = ((bf16[1,64,128]{2,0,1:T(2,128)(2,1)}), bf16[1,64,128]{2,0,1:T(2,128)(2,1)S(1)}, u32[]{:S(2)}, u32[]{:S(2)}) async-start(bf16[1,64,128]{2,0,1:T(2,128)(2,1)} %copy.56), calls=%async_computation.1 | async-start | bytes 65536 | tf_op jit(solution)/shard_map/all_to_all | solution.py:64
  112.0 24.0 %gather_fusion = bf16[8192,24]{1,0:T(8,128)(2,1)S(1)} fusion(bf16[24,4096]{0,1:T(8,128)(2,1)S(1)} %bitcast.53, s32[8192]{0:T(1024)S(1)} %broadcast_clamp_fusion), kind=kCustom, calls=%fused_computation | custom fusion | bytes 819200 | tf_op jit(solution)/shard_map/jit(_take)/gather | solution.py:58
  136.0 0.9 copy.54
  137.0 0.9 select_select_fusion
  137.8 10.3 %all-to-all-start = ((bf16[24,64,128]{2,0,1:T(8,128)(2,1)}), bf16[24,64,128]{2,0,1:T(8,128)(2,1)S(1)}, u32[]{:S(2)}, u32[]{:S(2)}) async-start(bf16[24,64,128]{2,0,1:T(8,128)(2,1)} %select_select_fusion), calls=%async_computation | async-start | bytes 786432 | tf_op jit(solution)/shard_map/all_to_all | solution.py:63
  148.3 1.2 fusion.29
  149.6 13.2 %all-to-all-done = bf16[24,64,128]{2,0,1:T(8,128)(2,1)S(1)} async-done(((bf16[24,64,128]{2,0,1:T(8,128)(2,1)}), bf16[24,64,128]{2,0,1:T(8,128)(2,1)S(1)}, u32[]{:S(2)}, u32[]{:S(2)}) %all-to-all-start) | async-done | bytes 393248 | tf_op jit(solution)/shard_map/all_to_all | solution.py:63
  162.7 6.2 %all-to-all-start.2 = ((s32[1,64,128]{2,0,1:T(1,128)}), s32[1,64,128]{2,0,1:T(1,128)S(1)}, u32[]{:S(2)}, u32[]{:S(2)}) async-start(s32[1,64,128]{2,0,1:T(1,128)} %bitcast.11), calls=%async_computation.2 | async-start | bytes 65536 | tf_op jit(solution)/shard_map/all_to_all | solution.py:65
  169.5 8.8 %all-to-all-done.2 = s32[1,64,128]{2,0,1:T(1,128)S(1)} async-done(((s32[1,64,128]{2,0,1:T(1,128)}), s32[1,64,128]{2,0,1:T(1,128)S(1)}, u32[]{:S(2)}, u32[]{:S(2)}) %all-to-all-start.2) | async-done | bytes 32800 | tf_op jit(solution)/shard_map/all_to_all | solution.py:65
  178.3 35.6 %while.14 = (s32[]{:T(128)}, f32[192,2048]{1,0:T(8,128)}, bf16[192,8192]{1,0:T(8,128)(2,1)S(1)}, s32[8192]{0:T(1024)S(1)}, s32[]{:T(128)}, /*index=5*/s32[]{:T(128)}, s32[]{:T(128)}, s32[]{:T(128)}) while((s32[]{:T(128)}, f32[192,2048]{1,0:T(8,128)}, bf16[192,8192]{1,0:T(8,128)(2,1)S(1)}, s32[8192]{0:T(1024)S(1)}, s32[]{:T(128)}, ...), condition=%wide.region_1.2_spmd.clone, body=%wide.region_0.1_spmd.clone.sunk | while | flops 808189952 | bytes 3551381 | solution.py:82
  178.3 3.2 fusion.57
  181.5 4.6 %fusion.57 = f32[192,2048]{1,0:T(8,128)} fusion(s32[1024]{0:T(1024)S(1)} %dynamic_slice.21, f32[192,2048]{1,0:T(8,128)} %get-tuple-element.167, pred[]{:T(512)S(6)} %compare.3, bf16[192,8192]{1,0:T(8,128)(2,1)S(1)} %get-tuple-element.176, s32[]{:T(128)S(6)} %select_n.102), kind=kOutput, calls=%fused_computation.7.clone.1 | convolution fusion | flops 808189952 | bytes 3543045 | tf_op jit(solution)/shard_map/while/body/eval_jaxpr/dot_general | solution.py:80
  186.2 4.6 %fusion.57 = f32[192,2048]{1,0:T(8,128)} fusion(s32[1024]{0:T(1024)S(1)} %dynamic_slice.21, f32[192,2048]{1,0:T(8,128)} %get-tuple-element.167, pred[]{:T(512)S(6)} %compare.3, bf16[192,8192]{1,0:T(8,128)(2,1)S(1)} %get-tuple-element.176, s32[]{:T(128)S(6)} %select_n.102), kind=kOutput, calls=%fused_computation.7.clone.1 | convolution fusion | flops 808189952 | bytes 3543045 | tf_op jit(solution)/shard_map/while/body/eval_jaxpr/dot_general | solution.py:80
  190.8 4.6 %fusion.57 = f32[192,2048]{1,0:T(8,128)} fusion(s32[1024]{0:T(1024)S(1)} %dynamic_slice.21, f32[192,2048]{1,0:T(8,128)} %get-tuple-element.167, pred[]{:T(512)S(6)} %compare.3, bf16[192,8192]{1,0:T(8,128)(2,1)S(1)} %get-tuple-element.176, s32[]{:T(128)S(6)} %select_n.102), kind=kOutput, calls=%fused_computation.7.clone.1 | convolution fusion | flops 808189952 | bytes 3543045 | tf_op jit(solution)/shard_map/while/body/eval_jaxpr/dot_general | solution.py:80
  195.4 4.6 %fusion.57 = f32[192,2048]{1,0:T(8,128)} fusion(s32[1024]{0:T(1024)S(1)} %dynamic_slice.21, f32[192,2048]{1,0:T(8,128)} %get-tuple-element.167, pred[]{:T(512)S(6)} %compare.3, bf16[192,8192]{1,0:T(8,128)(2,1)S(1)} %get-tuple-element.176, s32[]{:T(128)S(6)} %select_n.102), kind=kOutput, calls=%fused_computation.7.clone.1 | convolution fusion | flops 808189952 | bytes 3543045 | tf_op jit(solution)/shard_map/while/body/eval_jaxpr/dot_general | solution.py:80
  200.1 4.6 %fusion.57 = f32[192,2048]{1,0:T(8,128)} fusion(s32[1024]{0:T(1024)S(1)} %dynamic_slice.21, f32[192,2048]{1,0:T(8,128)} %get-tuple-element.167, pred[]{:T(512)S(6)} %compare.3, bf16[192,8192]{1,0:T(8,128)(2,1)S(1)} %get-tuple-element.176, s32[]{:T(128)S(6)} %select_n.102), kind=kOutput, calls=%fused_computation.7.clone.1 | convolution fusion | flops 808189952 | bytes 3543045 | tf_op jit(solution)/shard_map/while/body/eval_jaxpr/dot_general | solution.py:80
  204.7 4.6 %fusion.57 = f32[192,2048]{1,0:T(8,128)} fusion(s32[1024]{0:T(1024)S(1)} %dynamic_slice.21, f32[192,2048]{1,0:T(8,128)} %get-tuple-element.167, pred[]{:T(512)S(6)} %compare.3, bf16[192,8192]{1,0:T(8,128)(2,1)S(1)} %get-tuple-element.176, s32[]{:T(128)S(6)} %select_n.102), kind=kOutput, calls=%fused_computation.7.clone.1 | convolution fusion | flops 808189952 | bytes 3543045 | tf_op jit(solution)/shard_map/while/body/eval_jaxpr/dot_general | solution.py:80
  209.3 4.6 %fusion.57 = f32[192,2048]{1,0:T(8,128)} fusion(s32[1024]{0:T(1024)S(1)} %dynamic_slice.21, f32[192,2048]{1,0:T(8,128)} %get-tuple-element.167, pred[]{:T(512)S(6)} %compare.3, bf16[192,8192]{1,0:T(8,128)(2,1)S(1)} %get-tuple-element.176, s32[]{:T(128)S(6)} %select_n.102), kind=kOutput, calls=%fused_computation.7.clone.1 | convolution fusion | flops 808189952 | bytes 3543045 | tf_op jit(solution)/shard_map/while/body/eval_jaxpr/dot_general | solution.py:80
  214.0 1.5 convert_bitcast_fusion.1
  215.9 40.7 %all_to_all.28 = bf16[4,24,8,2048]{3,2,1,0:T(8,128)(2,1)S(1)} all-to-all(bf16[4,24,8,2048]{3,2,1,0:T(8,128)(2,1)S(1)} %stack.3), channel_id=1, replica_groups=mesh['band'=64,'lev'=4] {'lev'}, dimensions={0} | all-to-all | bytes 6291456 | tf_op jit(solution)/shard_map/all_to_all | solution.py:41
  256.5 5.2 %copy.58 = bf16[96,8,2048]{0,1,2:T(8,128)(2,1)} copy(bf16[96,8,2048]{2,1,0:T(8,128)(2,1)S(1)} %bitcast.54) | data formatting | bytes 6291456 | tf_op jit(solution)/shard_map/reshape | solution.py:40
  261.7 6.8 %all-to-all-start.4 = ((bf16[96,8,2048]{0,1,2:T(8,128)(2,1)}), bf16[96,8,2048]{0,1,2:T(8,128)(2,1)}, u32[]{:S(2)}, u32[]{:S(2)}) async-start(bf16[96,8,2048]{0,1,2:T(8,128)(2,1)} %copy.58), calls=%async_computation.4 | async-start | bytes 8388608 | tf_op jit(solution)/shard_map/all_to_all | solution.py:90
  268.6 95.9 %all-to-all-done.4 = bf16[96,8,2048]{0,1,2:T(8,128)(2,1)} async-done(((bf16[96,8,2048]{0,1,2:T(8,128)(2,1)}), bf16[96,8,2048]{0,1,2:T(8,128)(2,1)}, u32[]{:S(2)}, u32[]{:S(2)}) %all-to-all-start.4) | async-done | bytes 3145760 | tf_op jit(solution)/shard_map/all_to_all | solution.py:90
  364.5 13.4 %copy.60 = bf16[96,8,64,32]{2,3,1,0:T(8,128)(2,1)} copy(bf16[96,8,64,32]{0,1,3,2:T(8,128)(2,1)} %bitcast.15) | data formatting | bytes 6291456 | tf_op jit(solution)/shard_map/reshape | solution.py:92
  377.8 11.2 %multiply_reduce_fusion = (f32[32,512]{1,0:T(8,128)S(1)}, bf16[96,32,512]{2,1,0:T(8,128)(2,1)}) fusion(bf16[96,8,64,32]{2,3,1,0:T(8,128)(2,1)} %copy.60, f32[64,8]{0,1:T(8,128)S(1)} %add_add_fusion, f32[512]{0:T(512)S(1)} %get-tuple-element.131, f32[512]{0:T(512)S(1)} %get-tuple-element.132), kind=kOutput, calls=%fused_computation.20 | convolution fusion | flops 1617936384 | bytes 6363136 | tf_op jit(solution)/shard_map/cjbm,kbj->cmk/dot_general | solution.py:94
  389.1 12.7 %fusion.20 = bf16[64,32,512]{2,0,1:T(8,128)(2,1)S(1)} fusion(f32[64]{0:T(128)S(1)} %copy-done.8, f32[256]{0:T(256)S(1)} %copy-done.7, f32[32,512]{1,0:T(8,128)S(1)} %add_rsqrt_fusion, bf16[96,32,512]{2,1,0:T(8,128)(2,1)} %get-tuple-element.128, bf16[96,256]{1,0:T(8,128)(2,1)S(1)} %copy-done, bf16[256,64]{0,1:T(8,128)(2,1)S(1)} %copy-done.6), kind=kOutput, calls=%fused_computation.26 | convolution fusion | flops 1390411776 | bytes 5391616 | tf_op jit(solution)/shard_map/ho,hmk->omk/dot_general | solution.py:103
  401.8 2.5 copy.63
  (43 shorter events, 1.8 us)
Async XLA Ops:
  0.0 389.0 %copy-start = (bf16[96,256]{1,0:T(8,128)(2,1)S(1)}, bf16[96,256]{1,0:T(8,128)(2,1)}, u32[]{:S(2)}) copy-start(bf16[96,256]{1,0:T(8,128)(2,1)} %param.16) | copy-start | bytes 147460
  0.0 0.8 copy-start.1
  0.8 45.6 %copy-start.3 = (s32[1,64,128]{2,1,0:T(8,128)S(1)}, s32[1,64,128]{2,1,0:T(8,128)}, u32[]{:S(2)}) copy-start(s32[1,64,128]{2,1,0:T(8,128)} %param.14) | copy-start | bytes 98308
  46.4 0.7 copy-start.2
  47.1 64.4 %copy-start.4 = (bf16[1,24,4096]{2,1,0:T(8,128)(2,1)S(1)}, bf16[1,24,4096]{2,1,0:T(8,128)(2,1)}, u32[]{:S(2)}) copy-start(bf16[1,24,4096]{2,1,0:T(8,128)(2,1)} %param.11) | copy-start | bytes 589828
  97.8 39.0 %copy-start.5 = (s32[1,64]{1,0:T(1,128)S(1)}, s32[1,64]{1,0:T(1,128)}, u32[]{:S(2)}) copy-start(s32[1,64]{1,0:T(1,128)} %param.15) | copy-start | bytes 772
  98.5 39.4 %all-to-all-start.1 = ((bf16[1,64,128]{2,0,1:T(2,128)(2,1)}), bf16[1,64,128]{2,0,1:T(2,128)(2,1)S(1)}, u32[]{:S(2)}, u32[]{:S(2)}) async-start(bf16[1,64,128]{2,0,1:T(2,128)(2,1)} %copy.56), calls=%async_computation.1 | async-start | bytes 65536 | tf_op jit(solution)/shard_map/all_to_all | solution.py:64
  137.8 24.9 %all-to-all-start = ((bf16[24,64,128]{2,0,1:T(8,128)(2,1)}), bf16[24,64,128]{2,0,1:T(8,128)(2,1)S(1)}, u32[]{:S(2)}, u32[]{:S(2)}) async-start(bf16[24,64,128]{2,0,1:T(8,128)(2,1)} %select_select_fusion), calls=%async_computation | async-start | bytes 786432 | tf_op jit(solution)/shard_map/all_to_all | solution.py:63
  162.7 15.6 %all-to-all-start.2 = ((s32[1,64,128]{2,0,1:T(1,128)}), s32[1,64,128]{2,0,1:T(1,128)S(1)}, u32[]{:S(2)}, u32[]{:S(2)}) async-start(s32[1,64,128]{2,0,1:T(1,128)} %bitcast.11), calls=%async_computation.2 | async-start | bytes 65536 | tf_op jit(solution)/shard_map/all_to_all | solution.py:65
  261.7 102.7 %all-to-all-start.4 = ((bf16[96,8,2048]{0,1,2:T(8,128)(2,1)}), bf16[96,8,2048]{0,1,2:T(8,128)(2,1)}, u32[]{:S(2)}, u32[]{:S(2)}) async-start(bf16[96,8,2048]{0,1,2:T(8,128)(2,1)} %copy.58), calls=%async_computation.4 | async-start | bytes 8388608 | tf_op jit(solution)/shard_map/all_to_all | solution.py:90
  377.8 11.2 %copy-start.6 = (bf16[256,64]{0,1:T(8,128)(2,1)S(1)}, bf16[256,64]{0,1:T(8,128)(2,1)}, u32[]{:S(2)}) copy-start(bf16[256,64]{0,1:T(8,128)(2,1)} %param.18) | copy-start | bytes 98308
  377.8 11.2 %copy-start.7 = (f32[256]{0:T(256)S(1)}, f32[256]{0:T(256)}, u32[]{:S(2)}) copy-start(f32[256]{0:T(256)} %param.17) | copy-start | bytes 3076
  377.8 11.2 %copy-start.8 = (f32[64]{0:T(128)S(1)}, f32[64]{0:T(128)}, u32[]{:S(2)}) copy-start(f32[64]{0:T(128)} %param.19) | copy-start | bytes 772
